TPU v7x, 128 devices: a whole 4x4x4 slice. The times are simulated.
128 devices in a mesh: cuts: 8 (over y, core), fsdp: 16 (over z, x).
Axes of the slice: x: 4, y: 4, z: 4, core: 2. Of those that a mesh axis runs over, the one named last changes fastest.
Arguments:
- hidden_states: bfloat16 [65536, 8192], P(('cuts', 'fsdp')), may hold values from -1200 to 1200
- key_cotangent: bfloat16 [65536, 512], P(('cuts', 'fsdp')), may hold values from -60 to 60
- old_weight: bfloat16 [16384, 256], P(('cuts', 'fsdp')), may hold values from -0.0625 to 0.0625
- old_first: bfloat16 [16384, 256], P(('cuts', 'fsdp')), may hold values from -1 to 1
- old_first_scale: float32 [16384], P(('cuts', 'fsdp')), may hold values from 3e-05 to 0.0003
- old_second: bfloat16 [16384, 256], P(('cuts', 'fsdp')), may hold values from 0 to 1
- old_second_scale: float32 [16384], P(('cuts', 'fsdp')), may hold values from 1e-08 to 1e-07
- send_counts: int32 [128, 128], P(('cuts', 'fsdp')), may hold values from 0 to 2, as said below
Outputs:
- input_grad: bfloat16 [65536, 8192], P(('cuts', 'fsdp'))
- new_weight: bfloat16 [8192, 512], P(('cuts', 'fsdp'))
- first_code: bfloat16 [8192, 512], P(('cuts', 'fsdp'))
- first_scale: float32 [8192, 2], P(('cuts', 'fsdp'))
- second_code: bfloat16 [8192, 512], P(('cuts', 'fsdp'))
- second_scale: float32 [8192, 2], P(('cuts', 'fsdp'))
Inputs may be any that keep to these rules, and one draw needn't show every extreme that they name: Every row and every column of send_counts sums to 128; each entry is 0, 1 or 2, and every row and every column holds 2 exactly once.
All inputs are finite; a program needn't handle non-finite values.
Results may differ from a plain program's by a relative error of at most 0.00075.
Values may be sent and summed in bfloat16 or wider, within the bound.
A program may use at most 128 MiB of HBM per device.

v0:
```python
import jax
import jax.numpy as jnp
from jax import lax
from jax.sharding import PartitionSpec as P

STEP = 2000
beta_first = 0.9
beta_second = 0.95
adam_epsilon = 1e-05
learn_rate = 0.001
weight_decay = 0.1
clip_norm = 1.0
tiny_scale = 1e-30


def adam_blocks(clipped, weight, first, first_scale, second, second_scale):
    m_old = first.astype(jnp.float32) * first_scale[:, None]
    v_old = second.astype(jnp.float32) * second_scale[:, None]
    m_new = beta_first * m_old + (1.0 - beta_first) * clipped
    v_new = beta_second * v_old + (1.0 - beta_second) * clipped * clipped
    m_hat = m_new / (1.0 - beta_first**STEP)
    v_hat = v_new / (1.0 - beta_second**STEP)
    w_old = weight.astype(jnp.float32)
    w_new = (
        w_old - learn_rate * (m_hat / (jnp.sqrt(v_hat) + adam_epsilon) + weight_decay * w_old)
    ).astype(jnp.bfloat16)
    m_scale = jnp.max(jnp.abs(m_new), axis=1) + tiny_scale
    v_scale = jnp.max(v_new, axis=1) + tiny_scale
    m_code = (m_new / m_scale[:, None]).astype(jnp.bfloat16)
    v_code = (v_new / v_scale[:, None]).astype(jnp.bfloat16)
    return (w_new, m_code, m_scale, v_code, v_scale)


def shards(
    hidden_states,
    key_cotangent,
    old_weight,
    old_first,
    old_first_scale,
    old_second,
    old_second_scale,
    send_counts,
):
    peer_count = lax.axis_size(("cuts", "fsdp"))
    slot_count = old_weight.shape[0]
    block_size = old_weight.shape[1]
    key_width = key_cotangent.shape[1]
    peer_slots = 2 * slot_count // peer_count
    own_rows = slot_count * block_size // key_width
    row_counts = send_counts[0]
    slot_ends = jnp.cumsum(row_counts)
    starts = slot_ends - row_counts
    lane_index = jnp.arange(peer_slots, dtype=jnp.int32)
    live_slots = lane_index[None, :] < row_counts[:, None]
    pick_index = jnp.where(live_slots, starts[:, None] + lane_index[None, :], 0)
    stacked = jnp.stack([old_weight, old_first, old_second], axis=1)
    scales = jnp.stack([old_first_scale, old_second_scale], axis=1)
    packed = stacked[pick_index]
    packed_scales = scales[pick_index]
    tallies = row_counts.astype(jnp.float32)[:, None]
    arrived = lax.all_to_all(packed, ("cuts", "fsdp"), split_axis=0, concat_axis=0, tiled=True)
    arrived_scales, arrived_tallies = (
        lax.all_to_all(packed_scales, ("cuts", "fsdp"), split_axis=0, concat_axis=0, tiled=True),
        lax.all_to_all(tallies, ("cuts", "fsdp"), split_axis=0, concat_axis=0, tiled=True),
    )
    got_counts = arrived_tallies[:, 0].astype(jnp.int32)
    offsets = jnp.cumsum(got_counts) - got_counts
    live_here = lane_index[None, :] < got_counts[:, None]
    target = jnp.where(live_here, offsets[:, None] + lane_index[None, :], slot_count).reshape(-1)
    owned_state = (
        jnp.zeros((slot_count, 3, block_size), jnp.bfloat16)
        .at[target]
        .set(arrived.reshape(-1, 3, block_size), mode="drop")
    )
    owned_scales = (
        jnp.zeros((slot_count, 2), jnp.float32)
        .at[target]
        .set(arrived_scales.reshape(-1, 2), mode="drop")
    )
    own_weight = owned_state[:, 0].reshape(own_rows, key_width)
    input_grad = lax.dot_general(
        key_cotangent,
        lax.all_gather(own_weight, ("cuts", "fsdp"), axis=0, tiled=True),
        (((1,), (1,)), ((), ())),
        preferred_element_type=jnp.float32,
    ).astype(jnp.bfloat16)
    gradient = lax.psum_scatter(
        lax.dot_general(
            hidden_states,
            key_cotangent,
            (((0,), (0,)), ((), ())),
            preferred_element_type=jnp.float32,
        ),
        ("cuts", "fsdp"),
        scatter_dimension=0,
        tiled=True,
    )
    token_total = hidden_states.shape[0] * peer_count
    gradient = gradient / token_total
    square_sum = lax.psum(jnp.sum(gradient * gradient), ("cuts", "fsdp"))
    factor = jnp.minimum(1.0, clip_norm / (jnp.sqrt(square_sum) + 1e-06))
    clipped = (gradient * factor).reshape(slot_count, block_size)
    w_new, m_code, m_scale, v_code, v_scale = adam_blocks(
        clipped,
        owned_state[:, 0],
        owned_state[:, 1],
        owned_scales[:, 0],
        owned_state[:, 2],
        owned_scales[:, 1],
    )
    blocks_row = key_width // block_size
    return (
        input_grad,
        w_new.reshape(own_rows, key_width),
        m_code.reshape(own_rows, key_width),
        m_scale.reshape(own_rows, blocks_row),
        v_code.reshape(own_rows, key_width),
        v_scale.reshape(own_rows, blocks_row),
    )


def solution(mesh):
    placed = (
        P(("cuts", "fsdp"), None),
        P(("cuts", "fsdp"), None),
        P(("cuts", "fsdp"), None),
        P(("cuts", "fsdp"), None),
        P(("cuts", "fsdp")),
        P(("cuts", "fsdp"), None),
        P(("cuts", "fsdp")),
        P(("cuts", "fsdp"), None),
    )
    return jax.shard_map(
        shards,
        mesh=mesh,
        in_specs=placed,
        out_specs=(
            P(("cuts", "fsdp"), None),
            P(("cuts", "fsdp"), None),
            P(("cuts", "fsdp"), None),
            P(("cuts", "fsdp"), None),
            P(("cuts", "fsdp"), None),
            P(("cuts", "fsdp"), None),
        ),
        check_vma=False,
    )
```

profile of v0, /device:TPU:1, one launch (start us, length us, event | category | flops | bytes accessed | tf_op | source)
XLA Modules:
  0.0 894.5 jit_solution(2391013964506324690)
XLA Ops:
  7.2 0.7 convert_bitcast_fusion
  7.9 0.7 copy.60
  8.6 11.5 %all-to-all-start = ((f32[128,1,1]{2,1,0:T(1,128)}), f32[128,1,1]{2,1,0:T(1,128)S(1)}, u32[]{:S(2)}, u32[]{:S(2)}) async-start(f32[128,1,1]{2,1,0:T(1,128)} %copy.60), calls=%async_computation | async-start | bytes 131072 | tf_op jit(solution)/shard_map/all_to_all | solution.py:64
  20.1 0.8 copy.65
  20.9 0.2 reduce-window.17
  21.2 0.7 bitcast_subtract_fusion
  21.8 0.8 compare_select_fusion
  22.6 0.1 reshape.290
  22.7 0.9 copy.62
  23.7 0.9 copy.63
  24.6 0.9 copy.64
  25.6 0.5 pad_maximum_fusion
  26.1 1.2 gather_fusion
  27.2 1.1 copy.66
  28.3 1.5 all-to-all-done
  29.9 8.2 all-to-all-start.1
  38.2 0.2 reduce-window.16
  38.5 2.4 convert_reduce_fusion
  41.0 0.1 select_n.48
  41.1 9.7 %all-to-all-done.1 = bf16[128,2,3,256]{3,1,2,0:T(2,128)(2,1)S(1)} async-done(((bf16[128,2,3,256]{3,1,2,0:T(2,128)(2,1)}), bf16[128,2,3,256]{3,1,2,0:T(2,128)(2,1)S(1)}, u32[]{:S(2)}, u32[]{:S(2)}) %all-to-all-start.1) | async-done | bytes 393248 | tf_op jit(solution)/shard_map/all_to_all | solution.py:61
  50.9 0.2 copy.77
  51.1 7.3 scatter_fusion
  58.5 0.5 slice_convert_fusion
  59.0 0.7 reshape_squeeze.3
  59.7 11.7 %fusion.15 = f32[8192,512]{1,0:T(8,128)} fusion(bf16[512,8192]{1,0:T(8,128)(2,1)} %param.8, bf16[512,512]{1,0:T(8,128)(2,1)S(1)} %copy-done), kind=kOutput, calls=%fused_computation.49 | convolution fusion | flops 4294967296 | bytes 25690112 | tf_op jit(solution)/shard_map/dot_general | solution.py:88
  71.5 0.6 copy-done.3
  72.2 0.7 gather_fusion.1
  73.0 0.9 copy.71
  73.8 14.2 %all_to_all.16 = f32[128,2,2]{1,2,0:T(2,128)S(1)} all-to-all(f32[128,2,2]{1,2,0:T(2,128)S(1)} %copy.71), channel_id=1, replica_groups=mesh['cuts'=8,'fsdp'=16] {'cuts','fsdp'}, dimensions={0} | all-to-all | bytes 4096 | tf_op jit(solution)/shard_map/all_to_all | solution.py:63
  88.1 0.9 copy.78
  88.9 1.3 scatter_custom_fusion.1
  90.3 0.2 slice_reduce_fusion.1
  90.5 0.1 mul.112
  90.6 0.1 mul.113
  90.9 0.1 mul.124
  91.1 0.4 fusion.14
  91.6 34.0 %all-gather.2.cloned.1.call-done = bf16[8192,512]{1,0:T(8,128)(2,1)} async-done(((bf16[64,512]{1,0:T(8,128)(2,1)}), bf16[8192,512]{1,0:T(8,128)(2,1)}) %all-gather.2.cloned.1.call-update) | async-done | bytes 8388624 | tf_op jit(solution)/shard_map/all_gather | solution.py:83
  125.6 10.2 %fusion = bf16[512,8192]{0,1:T(8,128)(2,1)} fusion(bf16[8192,512]{1,0:T(8,128)(2,1)} %all-gather.2.cloned.1.call-done, bf16[512,512]{1,0:T(8,128)(2,1)S(1)} %copy-done), kind=kOutput, calls=%fused_computation.5 | convolution fusion | flops 4299161600 | bytes 17301504 | tf_op jit(solution)/shard_map/dot_general | solution.py:81
  135.8 640.2 %reduce-scatter.2.cloned.1.call-done = f32[64,512]{1,0:T(8,128)} async-done(((f32[8192,512]{1,0:T(8,128)}), f32[64,512]{1,0:T(8,128)}) %reduce-scatter.2.cloned.1.call-update) | async-done | bytes 131088 | tf_op jit(solution)/shard_map/reduce_scatter | solution.py:87
  776.0 1.5 multiply_reduce_fusion
  777.6 11.9 %copy.74 = bf16[512,8192]{1,0:T(8,128)(2,1)} copy(bf16[512,8192]{0,1:T(8,128)(2,1)} %fusion) | data formatting | bytes 16777216
  789.5 93.8 %psum.7 = f32[]{:T(128)} all-reduce(f32[]{:T(128)} %multiply_reduce_fusion), channel_id=1, replica_groups=mesh['cuts'=8,'fsdp'=16] {'cuts','fsdp'}, use_global_device_ids=true, to_apply=%region_6.7 | all-reduce | flops 1 | bytes 8 | tf_op jit(solution)/shard_map/psum | solution.py:100
  884.1 0.8 fusion.3
  884.9 0.2 fusion.6
  885.1 0.1 add.128
  885.2 0.6 copy.75
  886.2 0.6 copy.76
  887.0 0.8 divide_convert_fusion
  (36 shorter events, 1.4 us)
Async XLA Ops:
  7.2 52.6 %copy-start = (bf16[512,512]{1,0:T(8,128)(2,1)S(1)}, bf16[512,512]{1,0:T(8,128)(2,1)}, u32[]{:S(2)}) copy-start(bf16[512,512]{1,0:T(8,128)(2,1)} %param.9) | copy-start | bytes 1572868
  8.6 21.2 %all-to-all-start = ((f32[128,1,1]{2,1,0:T(1,128)}), f32[128,1,1]{2,1,0:T(1,128)S(1)}, u32[]{:S(2)}, u32[]{:S(2)}) async-start(f32[128,1,1]{2,1,0:T(1,128)} %copy.60), calls=%async_computation | async-start | bytes 131072 | tf_op jit(solution)/shard_map/all_to_all | solution.py:64
  29.9 21.0 %all-to-all-start.1 = ((bf16[128,2,3,256]{3,1,2,0:T(2,128)(2,1)}), bf16[128,2,3,256]{3,1,2,0:T(2,128)(2,1)S(1)}, u32[]{:S(2)}, u32[]{:S(2)}) async-start(bf16[128,2,3,256]{3,1,2,0:T(2,128)(2,1)} %copy.66), calls=%async_computation.1 | async-start | bytes 786432 | tf_op jit(solution)/shard_map/all_to_all | solution.py:61
  38.1 87.5 %all-gather.2.cloned.1.call-start = ((), (), s32[]{:S(2)}) async-start(), calls=%async_computation.4 | async-start | bytes 8454144 | tf_op jit(solution)/shard_map/all_gather | solution.py:83
  59.7 716.3 %reduce-scatter.2.cloned.1.call-start = ((), (), s32[]{:S(2)}) async-start(), calls=%async_computation.5 | async-start | bytes 16908288 | tf_op jit(solution)/shard_map/reduce_scatter | solution.py:87
  71.4 0.7 copy-start.3
  71.4 0.7 copy-start.4
  777.5 106.5 %copy-start.1 = (bf16[64,512]{1,0:T(8,128)(2,1)S(1)}, bf16[64,512]{1,0:T(8,128)(2,1)}, u32[]{:S(2)}) copy-start(bf16[64,512]{1,0:T(8,128)(2,1)} %reshape_squeeze.3) | copy-start | bytes 196612
  777.6 106.5 %copy-start.2 = (f32[64,512]{1,0:T(8,128)S(1)}, f32[64,512]{1,0:T(8,128)}, u32[]{:S(2)}) copy-start(f32[64,512]{1,0:T(8,128)} %reduce-scatter.2.cloned.1.call-done) | copy-start | bytes 393220
Sparse Core Ops, SparseCore 0:
  59.8 65.7 all-gather.1
  128.0 647.9 reduce-scatter.1
where the time goes:
time: 895 us
  waiting for transfers between devices  686 us (77%)
  blocking collectives  108 us (12%)
  local copies, waits for them, and re-layouts  34.3 us (4%)
  matrix products  21.9 us (2%)
  starting transfers between devices  19.8 us (2%)
  between operations  15.1 us (2%)
  other arithmetic  9.88 us (1%)
    reduce_scatter x1, waiting for transfers between devices, shards(): lax.psum_scatter(lax.dot_general(hidden_states, key_cotangent, (((0,), (0...  640 us
    psum x1, blocking collectives, shards(): square_sum = lax.psum(jnp.sum(gradient * gradient), ('cuts', 'fsdp'))  93.8 us
    all_gather x1, waiting for transfers between devices, shards(): lax.all_gather(own_weight, ('cuts', 'fsdp'), axis=0, tiled=True)  34 us
  transfers between devices with their start and end apart: 4, of which 4 were waited for; matrix products, arithmetic and copies ran while one was open for 4% of the time, Pallas kernels for 0%

commit v1 on v0

--- a/solution.py
+++ b/solution.py
@@ -80,7 +80,12 @@
     own_weight = owned_state[:, 0].reshape(own_rows, key_width)
     input_grad = lax.dot_general(
         key_cotangent,
-        lax.all_gather(own_weight, ("cuts", "fsdp"), axis=0, tiled=True),
+        jnp.concatenate(
+            lax.all_to_all(
+                jnp.stack([own_weight] * lax.axis_size(("cuts", "fsdp"))), ("cuts", "fsdp"), 0, 0
+            ),
+            axis=0,
+        ),
         (((1,), (1,)), ((), ())),
         preferred_element_type=jnp.float32,
     ).astype(jnp.bfloat16)

time: 895 us -> 834 us (0.932)
  waiting for transfers between devices: 686 us -> 626 us
  blocking collectives: 108 us -> 96.4 us
  starting transfers between devices: 19.8 us -> 29.7 us
    reduce_scatter x1, waiting for transfers between devices: 640 us -> 489 us  [shards(): lax.psum_scatter(lax.dot_general(hidden_states, key_cotangent, (((0,), (0...]
    all_to_all x0 -> x2, waiting for transfers between devices: none -> 122 us  [the longest x1 119 us: shards(): lax.all_to_all(jnp.stack([own_weight] * lax.axis_size(('cuts', 'fsdp'))),...]
    all_gather x1 -> x0, waiting for transfers between devices: 34 us -> none  [shards(): lax.all_gather(own_weight, ('cuts', 'fsdp'), axis=0, tiled=True)]
    all_to_all x1 -> x0, blocking collectives: 14.2 us -> none  [shards(): lax.all_to_all(packed_scales, ('cuts', 'fsdp'), split_axis=0, concat_axis...]
    all_to_all x0 -> x2, starting transfers between devices: none -> 12 us  [the longest x1 7.63 us: shards(): lax.all_to_all(jnp.stack([own_weight] * lax.axis_size(('cuts', 'fsdp'))),...]
  transfers between devices with their start and end apart: 4 -> 5, of which waited for: 4 -> 5; matrix products, arithmetic and copies ran while one was open for 4% -> 4% of each run, Pallas kernels for 0% -> 0%
where the time goes in v1:
time: 834 us; the launch traced here: 833 us
  waiting for transfers between devices  626 us (75%)
  blocking collectives  96.4 us (12%)
  local copies, waits for them, and re-layouts  36.3 us (4%)
  starting transfers between devices  29.7 us (4%)
  matrix products  21.9 us (3%)
  between operations  15.2 us (2%)
    reduce_scatter x1, waiting for transfers between devices, shards(): lax.psum_scatter(lax.dot_general(hidden_states, key_cotangent, (((0,), (0...  489 us
    all_to_all x1, waiting for transfers between devices, shards(): lax.all_to_all(jnp.stack([own_weight] * lax.axis_size(('cuts', 'fsdp'))),...  119 us
    psum x1, blocking collectives, shards(): square_sum = lax.psum(jnp.sum(gradient * gradient), ('cuts', 'fsdp'))  96.4 us
  transfers between devices with their start and end apart: 5, of which 5 were waited for; matrix products, arithmetic and copies ran while one was open for 4% of the time, Pallas kernels for 0%

profile of v1, /device:TPU:1, one launch (start us, length us, event | category | flops | bytes accessed | tf_op | source)
XLA Modules:
  0.0 833.0 jit_solution(112604125082609523)
XLA Ops:
  7.2 1.0 copy-done
  8.2 11.7 %fusion.15 = f32[8192,512]{1,0:T(8,128)} fusion(bf16[512,8192]{1,0:T(8,128)(2,1)} %param.8, bf16[512,512]{1,0:T(8,128)(2,1)S(1)} %copy-done), kind=kOutput, calls=%fused_computation.49 | convolution fusion | flops 4294967296 | bytes 25690112 | tf_op jit(solution)/shard_map/dot_general | solution.py:93
  19.9 0.6 copy-done.5
  20.5 0.7 copy.60
  21.3 11.5 %all-to-all-start = ((f32[128,1,1]{2,1,0:T(1,128)}), f32[128,1,1]{2,1,0:T(1,128)S(1)}, u32[]{:S(2)}, u32[]{:S(2)}) async-start(f32[128,1,1]{2,1,0:T(1,128)} %copy.60), calls=%async_computation | async-start | bytes 131072 | tf_op jit(solution)/shard_map/all_to_all | solution.py:64
  32.9 0.2 reduce-window.17
  33.3 0.1 reshape.296
  33.8 0.5 pad_maximum_fusion
  34.3 1.2 gather_fusion
  35.5 1.1 copy.66
  36.7 0.7 gather_fusion.1
  37.4 1.5 copy.71
  38.9 3.6 all-to-all-done
  42.5 6.2 all-to-all-start.1
  48.7 0.2 reduce-window.16
  49.0 2.4 convert_reduce_fusion
  51.5 0.1 select_n.48
  51.6 10.9 %all-to-all-done.1 = bf16[128,2,3,256]{3,1,2,0:T(2,128)(2,1)S(1)} async-done(((bf16[128,2,3,256]{3,1,2,0:T(2,128)(2,1)}), bf16[128,2,3,256]{3,1,2,0:T(2,128)(2,1)S(1)}, u32[]{:S(2)}, u32[]{:S(2)}) %all-to-all-start.1) | async-done | bytes 393248 | tf_op jit(solution)/shard_map/all_to_all | solution.py:61
  62.5 4.4 all-to-all-start.3
  66.9 0.2 copy.77
  67.2 7.3 scatter_fusion
  74.5 0.5 slice_convert_fusion
  75.1 2.6 all-to-all-done.3
  77.7 4.4 stack.28
  82.2 7.6 all-to-all-start.2
  89.8 0.9 copy.78
  90.7 1.2 scatter_custom_fusion.1
  91.9 0.2 slice_reduce_fusion.1
  92.0 0.1 mul.112
  92.2 0.1 mul.113
  92.3 0.1 mul.123
  92.5 0.1 mul.124
  92.7 0.4 fusion.14
  93.2 119.4 %all-to-all-done.2 = bf16[128,64,512]{2,1,0:T(8,128)(2,1)} async-done(((bf16[128,64,512]{2,1,0:T(8,128)(2,1)}), bf16[128,64,512]{2,1,0:T(8,128)(2,1)}, u32[]{:S(2)}, u32[]{:S(2)}) %all-to-all-start.2) | async-done | bytes 8388640 | tf_op jit(solution)/shard_map/all_to_all | solution.py:84
  212.5 10.2 %fusion = bf16[512,8192]{0,1:T(8,128)(2,1)} fusion(bf16[8192,512]{1,0:T(8,128)(2,1)} %bitcast.10, bf16[512,512]{1,0:T(8,128)(2,1)S(1)} %copy-done), kind=kOutput, calls=%fused_computation.5 | convolution fusion | flops 4299161600 | bytes 17301504 | tf_op jit(solution)/shard_map/dot_general | solution.py:81
  222.8 489.1 %reduce-scatter.2.cloned.1.call-done = f32[64,512]{1,0:T(8,128)} async-done(((f32[8192,512]{1,0:T(8,128)}), f32[64,512]{1,0:T(8,128)}) %reduce-scatter.2.cloned.1.call-update) | async-done | bytes 131088 | tf_op jit(solution)/shard_map/reduce_scatter | solution.py:92
  711.9 1.5 multiply_reduce_fusion
  713.5 11.9 %copy.74 = bf16[512,8192]{1,0:T(8,128)(2,1)} copy(bf16[512,8192]{0,1:T(8,128)(2,1)} %fusion) | data formatting | bytes 16777216
  725.4 96.4 %psum.7 = f32[]{:T(128)} all-reduce(f32[]{:T(128)} %multiply_reduce_fusion), channel_id=1, replica_groups=mesh['cuts'=8,'fsdp'=16] {'cuts','fsdp'}, use_global_device_ids=true, to_apply=%region_6.7 | all-reduce | flops 1 | bytes 8 | tf_op jit(solution)/shard_map/psum | solution.py:105
  822.6 0.8 fusion.3
  823.3 0.2 fusion.6
  823.5 0.1 add.128
  823.7 0.6 copy.75
  824.3 0.1 div.41
  824.5 0.1 add.131
  824.6 0.6 copy.76
  825.3 0.1 div.44
  825.4 0.7 divide_convert_fusion
  (43 shorter events, 1.4 us)
Async XLA Ops:
  7.2 1.0 copy-start
  7.2 704.7 %reduce-scatter.2.cloned.1.call-start = ((), (), s32[]{:S(2)}) async-start(), calls=%async_computation.5 | async-start | bytes 16908288 | tf_op jit(solution)/shard_map/reduce_scatter | solution.py:92
  19.9 0.7 copy-start.5
  19.9 13.6 %copy-start.2 = (bf16[128,256]{1,0:T(8,128)(2,1)S(1)}, bf16[128,256]{1,0:T(8,128)(2,1)}, u32[]{:S(2)}) copy-start(bf16[128,256]{1,0:T(8,128)(2,1)} %param.10) | copy-start | bytes 196612
  19.9 13.7 %copy-start.3 = (bf16[128,256]{1,0:T(8,128)(2,1)S(1)}, bf16[128,256]{1,0:T(8,128)(2,1)}, u32[]{:S(2)}) copy-start(bf16[128,256]{1,0:T(8,128)(2,1)} %param.11) | copy-start | bytes 196612
  19.9 13.8 %copy-start.4 = (bf16[128,256]{1,0:T(8,128)(2,1)S(1)}, bf16[128,256]{1,0:T(8,128)(2,1)}, u32[]{:S(2)}) copy-start(bf16[128,256]{1,0:T(8,128)(2,1)} %param.13) | copy-start | bytes 196612
  19.9 14.4 %copy-start.6 = (f32[128]{0:T(128)S(1)}, f32[128]{0:T(128)}, u32[]{:S(2)}) copy-start(f32[128]{0:T(128)} %param.14) | copy-start | bytes 1540
  19.9 14.4 %copy-start.7 = (f32[128]{0:T(128)S(1)}, f32[128]{0:T(128)}, u32[]{:S(2)}) copy-start(f32[128]{0:T(128)} %param.12) | copy-start | bytes 1540
  21.3 21.2 %all-to-all-start = ((f32[128,1,1]{2,1,0:T(1,128)}), f32[128,1,1]{2,1,0:T(1,128)S(1)}, u32[]{:S(2)}, u32[]{:S(2)}) async-start(f32[128,1,1]{2,1,0:T(1,128)} %copy.60), calls=%async_computation | async-start | bytes 131072 | tf_op jit(solution)/shard_map/all_to_all | solution.py:64
  42.5 20.0 %all-to-all-start.1 = ((bf16[128,2,3,256]{3,1,2,0:T(2,128)(2,1)}), bf16[128,2,3,256]{3,1,2,0:T(2,128)(2,1)S(1)}, u32[]{:S(2)}, u32[]{:S(2)}) async-start(bf16[128,2,3,256]{3,1,2,0:T(2,128)(2,1)} %copy.66), calls=%async_computation.1 | async-start | bytes 786432 | tf_op jit(solution)/shard_map/all_to_all | solution.py:61
  62.5 15.2 %all-to-all-start.3 = ((f32[128,2,2]{1,2,0:T(2,128)}), f32[128,2,2]{1,2,0:T(2,128)S(1)}, u32[]{:S(2)}, u32[]{:S(2)}) async-start(f32[128,2,2]{1,2,0:T(2,128)} %copy.71), calls=%async_computation.3 | async-start | bytes 262144 | tf_op jit(solution)/shard_map/all_to_all | solution.py:63
  82.2 130.4 %all-to-all-start.2 = ((bf16[128,64,512]{2,1,0:T(8,128)(2,1)}), bf16[128,64,512]{2,1,0:T(8,128)(2,1)}, u32[]{:S(2)}, u32[]{:S(2)}) async-start(bf16[128,64,512]{2,1,0:T(8,128)(2,1)} %stack.28), calls=%async_computation.2 | async-start | bytes 16777216 | tf_op jit(solution)/shard_map/all_to_all | solution.py:84
  713.5 109.1 %copy-start.1 = (f32[64,512]{1,0:T(8,128)S(1)}, f32[64,512]{1,0:T(8,128)}, u32[]{:S(2)}) copy-start(f32[64,512]{1,0:T(8,128)} %reduce-scatter.2.cloned.1.call-done) | copy-start | bytes 393220
Sparse Core Ops, SparseCore 0:
  20.1 691.8 reduce-scatter.1
